TPU v7x, 512 devices: a whole 4x4x16 slice. The times are simulated.
512 devices in a mesh: ctx: 64 (over z_lo, y, core), head: 8 (over z_hi, x).
Axes of the slice: x: 4, y: 4, z: 16 (z_hi: 2, z_lo: 8; z = z_hi * 8 + z_lo), core: 2. Of those that a mesh axis runs over, the one named last changes fastest.
Arguments:
- queries: bfloat16 [8192, 4096], P('ctx', 'head'), may hold values from -8 to 8
- keys: bfloat16 [8192, 1024], P('ctx', 'head'), may hold values from -6 to 6
- values: bfloat16 [8192, 1024], P('ctx', 'head'), may hold values from -6 to 6
- out_weight: bfloat16 [4096, 8192], P('head', 'ctx'), may hold values from -2.390625 to 2.390625
- block_order: int32 [128], replicated, may hold values from 0 to 127, as said below
Outputs:
- projected: bfloat16 [8192, 8192], P('ctx', 'head')
Inputs may be any that keep to these rules, and one draw needn't show every extreme that they name: `block_order`: slot blocks 2 s and 2 s + 1 hold the position blocks p and 127 - p for some p, and each position block is held by exactly one slot block.
All inputs are finite; a program needn't handle non-finite values.
Results may differ from a plain program's by a relative error of at most 0.018.
Values may be sent and summed in bfloat16 or wider, within the bound.
No kernel may reach another device: no remote copies, remote signals or barrier semaphores. Data moves between devices by JAX's collectives and lax.ppermute only.
A program may use at most 128 MiB of HBM per device.

v0:
```python
import math
import jax
import jax.numpy as jnp
from jax import lax
from jax.sharding import PartitionSpec as P


def slot_positions(block_order, offset, number, block_len):
    row_index = offset + jnp.arange(number, dtype=jnp.int32)
    which_block = row_index // block_len
    matches = which_block[:, None] == jnp.arange(block_order.shape[0], dtype=jnp.int32)[None, :]
    block_start = jnp.sum(jnp.where(matches, block_order[None, :], 0), axis=1)
    return block_start * block_len + row_index % block_len


def local(queries, keys, values, out_weight, block_order):
    tok_rows = queries.shape[0]
    head_size = keys.shape[1]
    local_heads = queries.shape[1] // head_size
    block_len = tok_rows // 2
    query_heads = queries.reshape(tok_rows, local_heads, head_size)
    query_pos = slot_positions(block_order, lax.axis_index("ctx") * tok_rows, tok_rows, block_len)
    scaling = 1.0 / math.sqrt(head_size)
    running_max = jnp.full((local_heads, tok_rows), -1e30, jnp.float32)
    key_piece = lax.all_gather(keys, "ctx", axis=0, tiled=True)
    value_piece = lax.all_gather(values, "ctx", axis=0, tiled=True)
    key_pos = slot_positions(block_order, jnp.int32(0), key_piece.shape[0], block_len)
    scores = (
        jnp.einsum("thd,sd->hts", query_heads, key_piece, preferred_element_type=jnp.float32)
        * scaling
    )
    visible = key_pos[None, None, :] <= query_pos[None, :, None]
    scores = jnp.where(visible, scores, -1e30)
    new_max = jnp.maximum(running_max, jnp.max(scores, axis=-1))
    weights_now = jnp.where(visible, jnp.exp(scores - new_max[..., None]), 0.0)
    new_sum = jnp.sum(weights_now, axis=-1)
    weights_b = weights_now.astype(jnp.bfloat16)
    new_accum = jnp.einsum(
        "hts,sd->htd", weights_b, value_piece, preferred_element_type=jnp.float32
    )
    attended = (new_accum / new_sum[..., None]).astype(jnp.bfloat16)
    piece = lax.all_gather(out_weight, "ctx", axis=1, tiled=True)
    weight_heads = piece.reshape(local_heads, head_size, piece.shape[1])
    partial_value = jnp.einsum(
        "htd,hdc->htc", attended, weight_heads, preferred_element_type=jnp.float32
    ).astype(jnp.bfloat16)
    partial_value = lax.optimization_barrier(partial_value)
    term = jnp.sum(partial_value.astype(jnp.float32), axis=0)
    summed = lax.psum_scatter(term.astype(jnp.bfloat16), "head", scatter_dimension=1, tiled=True)
    return summed


def solution(mesh):
    in_specs = (P("ctx", "head"), P("ctx", "head"), P("ctx", "head"), P("head", "ctx"), P())
    out_specs = P("ctx", "head")
    return jax.shard_map(local, mesh=mesh, in_specs=in_specs, out_specs=out_specs, check_vma=False)
```

profile of v0, /device:TPU:8, one launch (start us, length us, event | category | flops | bytes accessed | tf_op | source)
XLA Modules:
  0.0 563.2 jit_solution(5981867400463570871)
XLA Ops:
  6.5 0.0 copy-start
  6.5 0.0 all-gather.4.cloned.1.call-start
  6.5 0.7 all-gather.4.cloned.1.call-update
  7.3 0.0 all-gather.6.cloned.1.call-start
  7.3 0.7 all-gather.6.cloned.1.call-update
  8.0 0.0 all-gather.8.cloned.1.call-start
  8.1 0.7 all-gather.8.cloned.1.call-update
  8.7 0.0 reduce-scatter.2.cloned.1.call-start
  8.8 0.8 select_reduce_fusion.1
  9.7 3.2 select_reduce_fusion
  12.9 3.7 broadcast_compare_fusion
  16.6 117.2 %all-gather.4.cloned.1.call-done = bf16[8192,128]{1,0:T(8,128)(2,1)} async-done(((bf16[128,128]{1,0:T(8,128)(2,1)}), bf16[8192,128]{1,0:T(8,128)(2,1)}) %all-gather.4.cloned.1.call-update) | async-done | bytes 2097168 | tf_op jit(solution)/shard_map/all_gather | solution.py:25
  133.8 0.0 copy-done
  133.8 3.8 fusion
  137.6 0.0 copy-start.1
  137.6 5.7 %copy-done.1 = f32[8192,128,4]{1,0,2:T(8,128)} copy-done((f32[8192,128,4]{1,0,2:T(8,128)}, f32[8192,128,4]{1,0,2:T(8,128)S(1)}, u32[]{:S(2)}) %copy-start.1) | copy-done | bytes 16777240
  143.3 4.2 fusion.1
  147.5 105.0 %all-gather.6.cloned.1.call-done = bf16[8192,128]{1,0:T(8,128)(2,1)} async-done(((bf16[128,128]{1,0:T(8,128)(2,1)}), bf16[8192,128]{1,0:T(8,128)(2,1)}) %all-gather.6.cloned.1.call-update) | async-done | bytes 2097168 | tf_op jit(solution)/shard_map/all_gather | solution.py:26
  252.5 137.7 %all-gather.8.cloned.1.call-done = bf16[512,8192]{1,0:T(8,128)(2,1)} async-done(((bf16[512,128]{1,0:T(8,128)(2,1)}), bf16[512,8192]{1,0:T(8,128)(2,1)}) %all-gather.8.cloned.1.call-update) | async-done | bytes 8388624 | tf_op jit(solution)/shard_map/all_gather | solution.py:42
  390.3 15.4 %convolution_convert_fusion = bf16[4,128,8192]{2,1,0:T(8,128)(2,1)} fusion(bf16[4,128,8192]{2,1,0:T(8,128)(2,1)} %bitcast.42, bf16[8192,128]{1,0:T(8,128)(2,1)} %all-gather.6.cloned.1.call-done, f32[8192,128,4]{1,0,2:T(8,128)} %copy-done.1, f32[4,128]{1,0:T(4,128)S(1)} %broadcast_maximum_fusion, pred[128,8192]{0,1:T(8,128)(4,1)S(1)} %broadcast_compare_fusion, ...), kind=kOutput, calls=%fused_computation.3 | convolution fusion | flops 2172780544 | bytes 36704256 | tf_op jit(solution)/shard_map/htd,hdc->htc/dot_general | solution.py:44
  405.7 6.9 %reduce_sum.42 = bf16[128,8192]{1,0:T(8,128)(2,1)} reduce(bf16[4,128,8192]{2,1,0:T(8,128)(2,1)} %convolution_convert_fusion, bf16[]{:T(256)} %constant.69.clone.1), dimensions={0}, to_apply=%region_4.5 | reduce | flops 3145728 | bytes 10485762 | tf_op jit(solution)/shard_map/reduce_sum | solution.py:48
  412.6 0.0 reduce-scatter.2.cloned.1.call-update
  412.6 144.0 %reduce-scatter.2.cloned.1.call-done = bf16[128,1024]{1,0:T(8,128)(2,1)} async-done(((bf16[128,8192]{1,0:T(8,128)(2,1)}), bf16[128,1024]{1,0:T(8,128)(2,1)}) %reduce-scatter.2.cloned.1.call-update) | async-done | bytes 262160 | tf_op jit(solution)/shard_map/reduce_scatter | solution.py:49
  (5 shorter events, 0.0 us)
Async XLA Ops:
  6.5 127.3 %copy-start = (bf16[128,512]{1,0:T(8,128)(2,1)S(1)}, bf16[128,512]{1,0:T(8,128)(2,1)}, u32[]{:S(2)}) copy-start(bf16[128,512]{1,0:T(8,128)(2,1)} %param.5) | copy-start | bytes 393220
  6.5 127.3 %all-gather.4.cloned.1.call-start = ((), (), s32[]{:S(2)}) async-start(), calls=%async_computation.1 | async-start | bytes 2129920 | tf_op jit(solution)/shard_map/all_gather | solution.py:25
  7.3 245.3 %all-gather.6.cloned.1.call-start = ((), (), s32[]{:S(2)}) async-start(), calls=%async_computation.2 | async-start | bytes 2129920 | tf_op jit(solution)/shard_map/all_gather | solution.py:26
  8.0 382.3 %all-gather.8.cloned.1.call-start = ((), (), s32[]{:S(2)}) async-start(), calls=%async_computation.3 | async-start | bytes 8519680 | tf_op jit(solution)/shard_map/all_gather | solution.py:42
  8.7 547.9 %reduce-scatter.2.cloned.1.call-start = ((), (), s32[]{:S(2)}) async-start(), calls=%async_computation.4 | async-start | bytes 2359296 | tf_op jit(solution)/shard_map/reduce_scatter | solution.py:49
  137.6 5.7 %copy-start.1 = (f32[8192,128,4]{1,0,2:T(8,128)}, f32[8192,128,4]{1,0,2:T(8,128)S(1)}, u32[]{:S(2)}) copy-start(f32[8192,128,4]{1,0,2:T(8,128)S(1)} %get-tuple-element.6) | copy-start | bytes 50331652
Sparse Core Ops, SparseCore 0:
  9.5 124.2 all-gather.3
  136.0 116.4 all-gather.5
  254.6 135.6 all-gather.7
  412.7 143.8 reduce-scatter.1
where the time goes:
time: 563 us
  waiting for transfers between devices  506 us (90%)
  matrix products  19.2 us (3%)
  other arithmetic  18.8 us (3%)
  between operations  13.2 us (2%)
  local copies, waits for them, and re-layouts  5.7 us (1%)
    reduce_scatter x1, waiting for transfers between devices, local(): lax.psum_scatter(term.astype(jnp.bfloat16), 'head', scatter_dimension=1,...  144 us
    all_gather x1, waiting for transfers between devices, local(): piece = lax.all_gather(out_weight, 'ctx', axis=1, tiled=True)  138 us
    all_gather x1, waiting for transfers between devices, local(): key_piece = lax.all_gather(keys, 'ctx', axis=0, tiled=True)  117 us
    all_gather x1, waiting for transfers between devices, local(): value_piece = lax.all_gather(values, 'ctx', axis=0, tiled=True)  105 us
    dot_general x1, matrix products, local(): jnp.einsum('htd,hdc->htc', attended, weight_heads, preferred_element_type...  15.4 us
  transfers between devices with their start and end apart: 4, of which 4 were waited for; matrix products, arithmetic and copies ran while one was open for 3% of the time, Pallas kernels for 0%

commit v1 on v0

--- a/solution.py
+++ b/solution.py
@@ -23,7 +23,9 @@
     scaling = 1.0 / math.sqrt(head_size)
     running_max = jnp.full((local_heads, tok_rows), -1e30, jnp.float32)
     key_piece = lax.all_gather(keys, "ctx", axis=0, tiled=True)
-    value_piece = lax.all_gather(values, "ctx", axis=0, tiled=True)
+    value_piece = jnp.concatenate(
+        lax.all_to_all(jnp.stack([values] * lax.axis_size("ctx")), "ctx", 0, 0), axis=0
+    )
     key_pos = slot_positions(block_order, jnp.int32(0), key_piece.shape[0], block_len)
     scores = (
         jnp.einsum("thd,sd->hts", query_heads, key_piece, preferred_element_type=jnp.float32)

time: 563 us -> 488 us (0.87)
  the two profiles are of different devices: /device:TPU:8 before, /device:TPU:16 now
where the time goes in v1:
time: 488 us
  waiting for transfers between devices  413 us (85%)
  other arithmetic  18.8 us (4%)
  matrix products  18.6 us (4%)
  starting transfers between devices  16.1 us (3%)
  between operations  13.2 us (3%)
  local copies, waits for them, and re-layouts  8.36 us (2%)
    reduce_scatter x1, waiting for transfers between devices, local(): lax.psum_scatter(term.astype(jnp.bfloat16), 'head', scatter_dimension=1,...  145 us
    all_gather x1, waiting for transfers between devices, local(): key_piece = lax.all_gather(keys, 'ctx', axis=0, tiled=True)  142 us
    all_gather x1, waiting for transfers between devices, local(): piece = lax.all_gather(out_weight, 'ctx', axis=1, tiled=True)  124 us
    all_to_all x1, starting transfers between devices, local(): lax.all_to_all(jnp.stack([values] * lax.axis_size('ctx')), 'ctx', 0, 0)  16 us
    dot_general x1, matrix products, local(): jnp.einsum('htd,hdc->htc', attended, weight_heads, preferred_element_type...  14.8 us
  transfers between devices with their start and end apart: 4, of which 3 were waited for; matrix products, arithmetic and copies ran while one was open for 4% of the time, Pallas kernels for 0%

profile of v1, /device:TPU:16, one launch (start us, length us, event | category | flops | bytes accessed | tf_op | source)
XLA Modules:
  0.0 487.8 jit_solution(15463399714420570460)
XLA Ops:
  6.5 0.0 copy-start
  6.5 0.0 all-gather.3.cloned.1.call-start
  6.5 0.7 all-gather.3.cloned.1.call-update
  7.3 0.0 all-gather.5.cloned.1.call-start
  7.3 0.7 all-gather.5.cloned.1.call-update
  8.0 2.7 stack.2
  10.7 16.0 %all-to-all-start = ((bf16[64,128,128]{2,1,0:T(8,128)(2,1)}), bf16[64,128,128]{2,1,0:T(8,128)(2,1)S(1)}, u32[]{:S(2)}, u32[]{:S(2)}) async-start(bf16[64,128,128]{2,1,0:T(8,128)(2,1)} %stack.2), calls=%async_computation | async-start | bytes 4194304 | tf_op jit(solution)/shard_map/all_to_all | solution.py:27
  26.7 0.0 reduce-scatter.2.cloned.1.call-start
  26.8 0.8 select_reduce_fusion.1
  27.6 3.2 select_reduce_fusion
  30.9 3.7 broadcast_compare_fusion
  34.6 141.9 %all-gather.3.cloned.1.call-done = bf16[8192,128]{1,0:T(8,128)(2,1)} async-done(((bf16[128,128]{1,0:T(8,128)(2,1)}), bf16[8192,128]{1,0:T(8,128)(2,1)}) %all-gather.3.cloned.1.call-update) | async-done | bytes 2097168 | tf_op jit(solution)/shard_map/all_gather | solution.py:25
  176.5 0.0 copy-done
  176.5 3.8 fusion
  180.3 0.0 copy-start.1
  180.3 5.7 %copy-done.1 = f32[8192,128,4]{1,0,2:T(8,128)} copy-done((f32[8192,128,4]{1,0,2:T(8,128)}, f32[8192,128,4]{1,0,2:T(8,128)S(1)}, u32[]{:S(2)}) %copy-start.1) | copy-done | bytes 16777240
  186.0 4.2 fusion.1
  190.2 0.0 all-to-all-done
  190.2 124.5 %all-gather.5.cloned.1.call-done = bf16[512,8192]{1,0:T(8,128)(2,1)} async-done(((bf16[512,128]{1,0:T(8,128)(2,1)}), bf16[512,8192]{1,0:T(8,128)(2,1)}) %all-gather.5.cloned.1.call-update) | async-done | bytes 8388624 | tf_op jit(solution)/shard_map/all_gather | solution.py:44
  314.6 14.8 %convolution_convert_fusion = bf16[4,128,8192]{2,1,0:T(8,128)(2,1)} fusion(bf16[4,128,8192]{2,1,0:T(8,128)(2,1)} %bitcast.38, bf16[8192,128,1]{1,0,2:T(8,128)(2,1)S(1)} %bitcast.37, f32[8192,128,4]{1,0,2:T(8,128)} %copy-done.1, f32[4,128]{1,0:T(4,128)S(1)} %broadcast_maximum_fusion, pred[128,8192]{0,1:T(8,128)(4,1)S(1)} %broadcast_compare_fusion, ...), kind=kOutput, calls=%fused_computation.3 | convolution fusion | flops 2172780544 | bytes 36704256 | tf_op jit(solution)/shard_map/htd,hdc->htc/dot_general | solution.py:46
  329.5 6.9 %reduce_sum.42 = bf16[128,8192]{1,0:T(8,128)(2,1)} reduce(bf16[4,128,8192]{2,1,0:T(8,128)(2,1)} %convolution_convert_fusion, bf16[]{:T(256)} %constant.69.clone.1), dimensions={0}, to_apply=%region_4.5 | reduce | flops 3145728 | bytes 10485762 | tf_op jit(solution)/shard_map/reduce_sum | solution.py:50
  336.4 0.0 reduce-scatter.2.cloned.1.call-update
  336.4 144.9 %reduce-scatter.2.cloned.1.call-done = bf16[128,1024]{1,0:T(8,128)(2,1)} async-done(((bf16[128,8192]{1,0:T(8,128)(2,1)}), bf16[128,1024]{1,0:T(8,128)(2,1)}) %reduce-scatter.2.cloned.1.call-update) | async-done | bytes 262160 | tf_op jit(solution)/shard_map/reduce_scatter | solution.py:51
  (5 shorter events, 0.0 us)
Async XLA Ops:
  6.5 170.0 %copy-start = (bf16[128,512]{1,0:T(8,128)(2,1)S(1)}, bf16[128,512]{1,0:T(8,128)(2,1)}, u32[]{:S(2)}) copy-start(bf16[128,512]{1,0:T(8,128)(2,1)} %param.5) | copy-start | bytes 393220
  6.5 170.0 %all-gather.3.cloned.1.call-start = ((), (), s32[]{:S(2)}) async-start(), calls=%async_computation.2 | async-start | bytes 2129920 | tf_op jit(solution)/shard_map/all_gather | solution.py:25
  7.3 307.4 %all-gather.5.cloned.1.call-start = ((), (), s32[]{:S(2)}) async-start(), calls=%async_computation.3 | async-start | bytes 8519680 | tf_op jit(solution)/shard_map/all_gather | solution.py:44
  10.7 179.5 %all-to-all-start = ((bf16[64,128,128]{2,1,0:T(8,128)(2,1)}), bf16[64,128,128]{2,1,0:T(8,128)(2,1)S(1)}, u32[]{:S(2)}, u32[]{:S(2)}) async-start(bf16[64,128,128]{2,1,0:T(8,128)(2,1)} %stack.2), calls=%async_computation | async-start | bytes 4194304 | tf_op jit(solution)/shard_map/all_to_all | solution.py:27
  26.7 454.6 %reduce-scatter.2.cloned.1.call-start = ((), (), s32[]{:S(2)}) async-start(), calls=%async_computation.4 | async-start | bytes 2359296 | tf_op jit(solution)/shard_map/reduce_scatter | solution.py:51
  180.3 5.7 %copy-start.1 = (f32[8192,128,4]{1,0,2:T(8,128)}, f32[8192,128,4]{1,0,2:T(8,128)S(1)}, u32[]{:S(2)}) copy-start(f32[8192,128,4]{1,0,2:T(8,128)S(1)} %get-tuple-element.6) | copy-start | bytes 50331652
Sparse Core Ops, SparseCore 0:
  9.5 166.9 all-gather.2
  178.6 136.0 all-gather.4
  336.5 144.7 reduce-scatter.1
